TPU v7x, 512 devices: a whole 4x4x16 slice. The times are simulated.
512 devices in a mesh: gx: 64 (over z, y), gz: 8 (over x, core).
Axes of the slice: x: 4, y: 4, z: 16, core: 2. Of those that a mesh axis runs over, the one named last changes fastest.
Arguments:
- tokens: bfloat16 [4, 256, 64, 768], P(None, 'gx', 'gz'), may hold values from -60 to 60
- cross_qkv: bfloat16 [768, 2304], P(None, 'gx'), may hold values from -16 to 16
- cross_out: bfloat16 [768, 768], P('gx'), may hold values from -0.21875 to 0.21875
- depth_qkv: bfloat16 [768, 2304], P(None, 'gx'), may hold values from -16 to 16
- depth_out: bfloat16 [768, 768], P('gx'), may hold values from -0.21875 to 0.21875
- up_proj: bfloat16 [768, 3072], P(None, 'gz'), may hold values from -0.21875 to 0.21875
- down_proj: bfloat16 [3072, 768], P('gz'), may hold values from -0.109375 to 0.109375
- gains: float32 [3, 768], replicated, may hold values from 0.5 to 1.5
- head_weight: float32 [768], replicated, may hold values from -0.21875 to 0.21875
- head_bias: float32 [1], replicated, may hold values from -1 to 1
Outputs:
- features: bfloat16 [4, 256, 64, 768], P(None, 'gx', 'gz')
- geotime: float32 [4, 256, 64], P(None, 'gx', 'gz')
All inputs are finite; a program needn't handle non-finite values.
Results may differ from a plain program's by a relative error of at most 0.013.
Values may be sent and summed in bfloat16 or wider, within the bound.
A program may use at most 64 MiB of HBM per device.

v0:
```python
import math
import jax
import jax.numpy as jnp
from jax import lax
from jax.sharding import PartitionSpec as P

HDIM = 64
log_span = math.log(256.0)


def carried_in(shard, axis, combine, identity):
    peers, position = (lax.axis_size(axis), lax.axis_index(axis))
    everything = lax.all_gather(shard, axis)
    start = jnp.broadcast_to(jnp.asarray(identity, shard.dtype), shard.shape)

    def step(k, before):
        reached = k < position
        new = combine(before, everything[k])
        return jnp.where(reached, new, before)

    return lax.fori_loop(0, peers, step, start)


def encodings(inlines, crosslines, depths, cross_start, depth_start, model_width):
    pairs = model_width // 2
    index = jnp.arange(pairs)
    freq = math.pi * jnp.exp(-log_span * index.astype(jnp.float32) / pairs)
    which = index % 3
    inline_pos = jnp.arange(inlines).astype(jnp.float32)[:, None, None, None]
    cross_pos = (cross_start + jnp.arange(crosslines)).astype(jnp.float32)[None, :, None, None]
    depth_pos = (depth_start + jnp.arange(depths)).astype(jnp.float32)[None, None, :, None]
    zeros = jnp.zeros((inlines, crosslines, depths, pairs), jnp.float32)
    position = jnp.where(
        which == 0, inline_pos + zeros, jnp.where(which == 1, cross_pos + zeros, depth_pos + zeros)
    )
    angle = position * freq
    return jnp.stack([jnp.sin(angle), jnp.cos(angle)], -1).reshape(
        inlines, crosslines, depths, model_width
    )


def normalize(stream, gain):
    scale = lax.rsqrt(jnp.mean(stream * stream, -1, keepdims=True) + 1e-05)
    return (stream * scale * gain).astype(jnp.bfloat16)


def attend(queries, keys, values):
    scale = queries.shape[-1] ** (-0.5)
    scores = (
        jnp.einsum("...qe,...ke->...qk", queries, keys, preferred_element_type=jnp.float32) * scale
    )
    scores = scores - jnp.max(scores, -1, keepdims=True)
    expo = jnp.exp(scores)
    weights = (expo / jnp.sum(expo, -1, keepdims=True)).astype(jnp.bfloat16)
    mixed = jnp.einsum("...qk,...ke->...qe", weights, values, preferred_element_type=jnp.float32)
    return mixed.astype(jnp.bfloat16)


def attend_items(trio):
    return attend(trio[0], trio[1], trio[2])


def body(
    tokens,
    cross_qkv,
    cross_out,
    depth_qkv,
    depth_out,
    up_proj,
    down_proj,
    gains,
    head_weight,
    head_bias,
):
    inlines, cross_dev, depth_dev, model_width = tokens.shape
    tok_rows = inlines * cross_dev * depth_dev
    head_count = model_width // HDIM
    cross_group = lax.axis_size("gx")
    encoding = encodings(
        inlines,
        cross_dev,
        depth_dev,
        lax.axis_index("gx") * cross_dev,
        lax.axis_index("gz") * depth_dev,
        model_width,
    )
    stream = (tokens.astype(jnp.float32) + encoding).reshape(tok_rows, model_width)
    normed = normalize(stream, gains[0])
    packed = jnp.dot(
        normed,
        lax.all_gather(cross_qkv, "gx", axis=1, tiled=True),
        preferred_element_type=jnp.float32,
    ).astype(jnp.bfloat16)
    packed = packed.reshape(inlines, cross_dev, depth_dev, 3, head_count, HDIM)
    lined = jnp.transpose(packed, (3, 0, 2, 4, 1, 5))
    per_item = inlines * depth_dev * head_count // cross_group
    lined = lined.reshape(3, cross_group, per_item, cross_dev, HDIM)
    mixed = attend_items(
        (
            lax.all_to_all(lined[0], "gx", split_axis=0, concat_axis=2, tiled=True),
            lax.all_to_all(lined[1], "gx", split_axis=0, concat_axis=2, tiled=True),
            lax.all_to_all(lined[2], "gx", split_axis=0, concat_axis=2, tiled=True),
        )
    )
    mixed = lax.all_to_all(mixed, "gx", split_axis=2, concat_axis=0, tiled=True)
    mixed = jnp.transpose(
        mixed.reshape(inlines, depth_dev, head_count, cross_dev, HDIM), (0, 3, 1, 2, 4)
    ).reshape(tok_rows, model_width)
    columns = mixed
    stream = stream + jnp.dot(
        columns,
        lax.all_gather(cross_out, "gx", axis=0, tiled=True),
        preferred_element_type=jnp.float32,
    )
    normed = normalize(stream, gains[1])
    packed = jnp.dot(
        normed,
        lax.all_gather(depth_qkv, "gx", axis=1, tiled=True),
        preferred_element_type=jnp.float32,
    ).astype(jnp.bfloat16)
    packed = packed.reshape(inlines, cross_dev, depth_dev, 3, head_count, HDIM)
    lined = jnp.transpose(packed, (3, 0, 1, 4, 2, 5))
    all_keys, all_values = (
        lax.all_gather(lined[1], "gz", axis=3, tiled=True),
        lax.all_gather(lined[2], "gz", axis=3, tiled=True),
    )
    mixed = attend(lined[0], all_keys, all_values)
    mixed = jnp.transpose(mixed, (0, 1, 3, 2, 4)).reshape(tok_rows, model_width)
    columns = mixed
    stream = stream + jnp.dot(
        columns,
        lax.all_gather(depth_out, "gx", axis=0, tiled=True),
        preferred_element_type=jnp.float32,
    )
    normed = normalize(stream, gains[2])
    hidden = jax.nn.gelu(
        jnp.dot(
            lax.all_gather(normed, "gz", axis=0, tiled=True),
            up_proj,
            preferred_element_type=jnp.float32,
        )
    ).astype(jnp.bfloat16)
    stream = stream + lax.psum_scatter(
        jnp.dot(hidden, down_proj, preferred_element_type=jnp.float32).astype(jnp.bfloat16),
        "gz",
        scatter_dimension=0,
        tiled=True,
    ).astype(jnp.float32)
    features = stream.astype(jnp.bfloat16).reshape(inlines, cross_dev, depth_dev, model_width)
    thickness = jax.nn.softplus(
        jnp.dot(stream, head_weight, precision=lax.Precision.HIGHEST) + head_bias[0]
    )
    local_time = jnp.cumsum(thickness.reshape(inlines, cross_dev, depth_dev), axis=2)
    line_total = local_time[:, :, -1]
    carried = carried_in(
        line_total, "gz", lambda earlier, later: earlier + later, jnp.zeros_like(line_total)
    )
    geotime = local_time + carried[:, :, None]
    return (features, geotime)


def solution(mesh):
    return jax.shard_map(
        body,
        mesh=mesh,
        in_specs=(
            P(None, "gx", "gz", None),
            P(None, "gx"),
            P("gx", None),
            P(None, "gx"),
            P("gx", None),
            P(None, "gz"),
            P("gz", None),
            P(),
            P(),
            P(),
        ),
        out_specs=(P(None, "gx", "gz", None), P(None, "gx", "gz")),
        check_vma=False,
    )
```

profile of v0, /device:TPU:1, one launch (start us, length us, event | category | flops | bytes accessed | tf_op | source)
XLA Modules:
  0.0 772.2 jit_solution(6534772506447443359)
XLA Ops:
  7.2 0.7 all-gather.21.cloned.1.call-update
  8.0 0.7 all-gather.23.cloned.1.call-update
  8.7 0.7 all-gather.25.cloned.1.call-update
  9.5 0.8 fusion.41
  10.3 6.4 copy.57
  16.6 4.4 copy.58
  21.4 132.3 %all-gather.21.cloned.1.call-done = bf16[64,36,768]{2,1,0:T(8,128)(2,1)} async-done(((bf16[1,36,768]{2,1,0:T(8,128)(2,1)}), bf16[64,36,768]{2,1,0:T(8,128)(2,1)}) %all-gather.21.cloned.1.call-update) | async-done | bytes 3538960 | tf_op jit(solution)/shard_map/all_gather | solution.py:91
  153.7 6.2 reshape.159
  159.8 3.3 convolution_convert_fusion.1
  163.1 1.0 reshape.145
  164.1 1.1 fusion.53
  165.3 0.3 copy.61
  165.6 0.9 reshape.175
  166.5 8.7 %all-to-all-start.1 = ((bf16[64,2,768]{2,1,0:T(2,128)(2,1)}), bf16[64,2,768]{2,1,0:T(2,128)(2,1)S(1)}, u32[]{:S(2)}, u32[]{:S(2)}) async-start(bf16[64,2,768]{2,1,0:T(2,128)(2,1)} %reshape.175), calls=%async_computation.1 | async-start | bytes 393216 | tf_op jit(solution)/shard_map/all_to_all | solution.py:101
  175.2 0.3 copy.59
  175.5 0.9 reshape.173
  176.5 15.4 %all-to-all-done.1 = bf16[64,2,768]{2,1,0:T(2,128)(2,1)S(1)} async-done(((bf16[64,2,768]{2,1,0:T(2,128)(2,1)}), bf16[64,2,768]{2,1,0:T(2,128)(2,1)S(1)}, u32[]{:S(2)}, u32[]{:S(2)}) %all-to-all-start.1) | async-done | bytes 196640 | tf_op jit(solution)/shard_map/all_to_all | solution.py:101
  191.9 4.6 all-to-all-start
  196.5 0.3 copy.65
  196.8 0.9 reshape.171
  197.7 15.1 %all-to-all-done = bf16[64,2,768]{2,1,0:T(2,128)(2,1)S(1)} async-done(((bf16[64,2,768]{2,1,0:T(2,128)(2,1)}), bf16[64,2,768]{2,1,0:T(2,128)(2,1)S(1)}, u32[]{:S(2)}, u32[]{:S(2)}) %all-to-all-start) | async-done | bytes 196640 | tf_op jit(solution)/shard_map/all_to_all | solution.py:100
  212.9 4.6 all-to-all-start.2
  217.5 0.5 all-gather.27.cloned.1.call-update
  218.1 0.3 reshape.176
  218.5 0.3 reshape.174
  218.9 15.0 %all-to-all-done.2 = bf16[64,2,768]{2,1,0:T(2,128)(2,1)S(1)} async-done(((bf16[64,2,768]{2,1,0:T(2,128)(2,1)}), bf16[64,2,768]{2,1,0:T(2,128)(2,1)S(1)}, u32[]{:S(2)}, u32[]{:S(2)}) %all-to-all-start.2) | async-done | bytes 196640 | tf_op jit(solution)/shard_map/all_to_all | solution.py:102
  234.4 1.8 fusion.55
  236.2 1.7 fusion.27
  237.9 0.3 copy.69
  238.2 1.0 reshape.177
  239.2 4.6 all-to-all-start.3
  244.1 49.5 %all-gather.23.cloned.1.call-done = bf16[64,12,768]{2,1,0:T(8,128)(2,1)} async-done(((bf16[1,12,768]{2,1,0:T(8,128)(2,1)}), bf16[64,12,768]{2,1,0:T(8,128)(2,1)}) %all-gather.23.cloned.1.call-update) | async-done | bytes 1179664 | tf_op jit(solution)/shard_map/all_gather | solution.py:112
  293.6 2.2 reshape.161
  295.9 142.8 %all-gather.25.cloned.1.call-done = bf16[64,36,768]{2,1,0:T(8,128)(2,1)} async-done(((bf16[1,36,768]{2,1,0:T(8,128)(2,1)}), bf16[64,36,768]{2,1,0:T(8,128)(2,1)}) %all-gather.25.cloned.1.call-update) | async-done | bytes 3538960 | tf_op jit(solution)/shard_map/all_gather | solution.py:118
  438.7 6.2 reshape.163
  444.9 0.3 reshape.178
  445.5 0.3 reshape.150
  445.8 0.4 multiply_reduce_fusion.1
  446.2 0.7 copy-done.1
  447.0 3.3 convolution_convert_fusion
  450.3 1.0 reshape.151
  451.3 0.3 copy.84
  451.6 1.0 fusion.54
  452.6 0.5 all-gather.19.cloned.1.call-update
  453.2 122.6 %all-gather.27.cloned.1.call-done = bf16[64,12,768]{2,1,0:T(8,128)(2,1)} async-done(((bf16[1,12,768]{2,1,0:T(8,128)(2,1)}), bf16[64,12,768]{2,1,0:T(8,128)(2,1)}) %all-gather.27.cloned.1.call-update) | async-done | bytes 1179664 | tf_op jit(solution)/shard_map/all_gather | solution.py:132
  575.8 2.2 reshape.165
  578.1 44.5 %all-gather.17.cloned.1.call-done = bf16[1,4,4,12,64,64]{5,4,3,2,1,0:T(8,128)(2,1)} async-done(((bf16[1,4,4,12,8,64]{5,4,3,2,1,0:T(8,128)(2,1)}), bf16[1,4,4,12,64,64]{5,4,3,2,1,0:T(8,128)(2,1)}) %all-gather.17.cloned.1.call-update) | async-done | bytes 1572880 | tf_op jit(solution)/shard_map/all_gather | solution.py:124
  622.5 4.6 fusion.56
  627.2 37.7 %all-gather.19.cloned.1.call-done = bf16[1,4,4,12,64,64]{5,4,3,2,1,0:T(8,128)(2,1)} async-done(((bf16[1,4,4,12,8,64]{5,4,3,2,1,0:T(8,128)(2,1)}), bf16[1,4,4,12,64,64]{5,4,3,2,1,0:T(8,128)(2,1)}) %all-gather.19.cloned.1.call-update) | async-done | bytes 1572880 | tf_op jit(solution)/shard_map/all_gather | solution.py:125
  664.9 3.1 fusion.24
  668.2 0.3 reshape.152
  668.5 0.6 copy-done.2
  669.0 0.4 multiply_reduce_fusion
  669.5 0.8 multiply_convert_fusion
  670.3 33.1 %all-gather.15.cloned.1.call-done = bf16[1024,768]{1,0:T(8,128)(2,1)} async-done(((bf16[128,768]{1,0:T(8,128)(2,1)}), bf16[1024,768]{1,0:T(8,128)(2,1)}) %all-gather.15.cloned.1.call-update) | async-done | bytes 1572880 | tf_op jit(solution)/shard_map/all_gather | solution.py:138
  703.5 4.6 convolution_convert_fusion.2
  708.2 0.7 copy-done.6
  709.5 37.5 %reduce-scatter.2.cloned.1.call-done = bf16[128,768]{1,0:T(8,128)(2,1)} async-done(((bf16[1024,768]{1,0:T(8,128)(2,1)}), bf16[128,768]{1,0:T(8,128)(2,1)}) %reduce-scatter.2.cloned.1.call-update) | async-done | bytes 196624 | tf_op jit(solution)/shard_map/reduce_scatter | solution.py:143
  747.0 1.4 compare_select_fusion
  748.4 0.7 reduce_window_sum.11
  749.3 13.5 %all-gather.2 = f32[32,4,1]{1,2,0:T(1,128)S(1)} all-gather(f32[4,4,1]{1,2,0:T(1,128)S(1)} %copy.75), channel_id=4, replica_groups=mesh['gx'=64,'gz'=8] {'gz'}, dimensions={0}, use_global_device_ids=true | all-gather | bytes 576 | tf_op jit(solution)/shard_map/all_gather | solution.py:13
  762.8 0.3 while.14
  763.1 0.7 broadcast_add_fusion
  763.8 1.6 fusion.37
  (56 shorter events, 2.5 us)
Async XLA Ops:
  7.2 696.3 %copy-start = (bf16[384,768]{1,0:T(8,128)(2,1)S(1)}, bf16[384,768]{1,0:T(8,128)(2,1)}, u32[]{:S(2)}) copy-start(bf16[384,768]{1,0:T(8,128)(2,1)} %param.18) | copy-start | bytes 1769476
  7.2 146.5 %all-gather.21.cloned.1.call-start = ((), (), s32[]{:S(2)}) async-start(), calls=%async_computation.9 | async-start | bytes 3993600 | tf_op jit(solution)/shard_map/all_gather | solution.py:91
  7.9 285.7 %all-gather.23.cloned.1.call-start = ((), (), s32[]{:S(2)}) async-start(), calls=%async_computation.10 | async-start | bytes 1597440 | tf_op jit(solution)/shard_map/all_gather | solution.py:112
  8.7 430.0 %all-gather.25.cloned.1.call-start = ((), (), s32[]{:S(2)}) async-start(), calls=%async_computation.11 | async-start | bytes 3993600 | tf_op jit(solution)/shard_map/all_gather | solution.py:118
  16.6 4.4 copy-start.4
  16.6 4.6 copy-start.5
  165.2 10.0 %copy-start.3 = (bf16[1,4,8,12,4,64]{5,3,0,2,4,1:T(8,128)(2,1)S(1)}, bf16[1,4,8,12,4,64]{5,3,0,2,4,1:T(8,128)(2,1)}, u32[]{:S(2)}) copy-start(bf16[1,4,8,12,4,64]{5,3,0,2,4,1:T(8,128)(2,1)} %get-tuple-element.128) | copy-start | bytes 589828
  166.5 25.4 %all-to-all-start.1 = ((bf16[64,2,768]{2,1,0:T(2,128)(2,1)}), bf16[64,2,768]{2,1,0:T(2,128)(2,1)S(1)}, u32[]{:S(2)}, u32[]{:S(2)}) async-start(bf16[64,2,768]{2,1,0:T(2,128)(2,1)} %reshape.175), calls=%async_computation.1 | async-start | bytes 393216 | tf_op jit(solution)/shard_map/all_to_all | solution.py:101
  191.9 21.0 %all-to-all-start = ((bf16[64,2,768]{2,1,0:T(2,128)(2,1)}), bf16[64,2,768]{2,1,0:T(2,128)(2,1)S(1)}, u32[]{:S(2)}, u32[]{:S(2)}) async-start(bf16[64,2,768]{2,1,0:T(2,128)(2,1)} %reshape.173), calls=%async_computation | async-start | bytes 393216 | tf_op jit(solution)/shard_map/all_to_all | solution.py:100
  212.9 21.1 %all-to-all-start.2 = ((bf16[64,2,768]{2,1,0:T(2,128)(2,1)}), bf16[64,2,768]{2,1,0:T(2,128)(2,1)S(1)}, u32[]{:S(2)}, u32[]{:S(2)}) async-start(bf16[64,2,768]{2,1,0:T(2,128)(2,1)} %reshape.171), calls=%async_computation.2 | async-start | bytes 393216 | tf_op jit(solution)/shard_map/all_to_all | solution.py:102
  217.5 358.3 %all-gather.27.cloned.1.call-start = ((), (), s32[]{:S(2)}) async-start(), calls=%async_computation.12 | async-start | bytes 1597440 | tf_op jit(solution)/shard_map/all_gather | solution.py:132
  239.2 205.6 %all-to-all-start.3 = ((bf16[64,2,768]{2,1,0:T(2,128)(2,1)}), bf16[64,2,768]{2,1,0:T(2,128)(2,1)S(1)}, u32[]{:S(2)}, u32[]{:S(2)}) async-start(bf16[64,2,768]{2,1,0:T(2,128)(2,1)} %reshape.177), calls=%async_computation.3 | async-start | bytes 393216 | tf_op jit(solution)/shard_map/all_to_all | solution.py:105
  243.9 378.7 %all-gather.17.cloned.1.call-start = ((), (), s32[]{:S(2)}) async-start(), calls=%async_computation.7 | async-start | bytes 3538944 | tf_op jit(solution)/shard_map/all_gather | solution.py:124
  446.2 0.7 copy-start.1
  452.6 212.3 %all-gather.19.cloned.1.call-start = ((), (), s32[]{:S(2)}) async-start(), calls=%async_computation.8 | async-start | bytes 3538944 | tf_op jit(solution)/shard_map/all_gather | solution.py:125
  453.2 250.3 %all-gather.15.cloned.1.call-start = ((), (), s32[]{:S(2)}) async-start(), calls=%async_computation.5 | async-start | bytes 1769472 | tf_op jit(solution)/shard_map/all_gather | solution.py:138
  668.0 1.0 copy-start.2
  670.3 76.7 %reduce-scatter.2.cloned.1.call-start = ((), (), s32[]{:S(2)}) async-start(), calls=%async_computation.6 | async-start | bytes 1769472 | tf_op jit(solution)/shard_map/reduce_scatter | solution.py:143
  708.1 0.7 copy-start.6
Sparse Core Ops, SparseCore 0:
  11.0 142.6 all-gather.20
  156.6 136.9 all-gather.22
  296.6 142.0 all-gather.24
  441.5 134.2 all-gather.26
  577.8 44.7 all-gather.16
  624.5 40.3 all-gather.18
  670.4 33.0 all-gather.14
  708.3 38.6 reduce-scatter.1
where the time goes:
time: 773 us; the launch traced here: 772 us
  waiting for transfers between devices  649 us (84%)
  local copies, waits for them, and re-layouts  41.9 us (5%)
  matrix products  24.7 us (3%)
  starting transfers between devices  23.1 us (3%)
  between operations  15.2 us (2%)
  blocking collectives  13.5 us (2%)
    all_gather x1, waiting for transfers between devices, body(): lax.all_gather(depth_qkv, 'gx', axis=1, tiled=True)  143 us
    all_gather x1, waiting for transfers between devices, body(): lax.all_gather(cross_qkv, 'gx', axis=1, tiled=True)  132 us
    all_gather x1, waiting for transfers between devices, body(): lax.all_gather(depth_out, 'gx', axis=0, tiled=True)  123 us
    all_gather x1, waiting for transfers between devices, body(): lax.all_gather(cross_out, 'gx', axis=0, tiled=True)  49.5 us
    all_gather x1, waiting for transfers between devices, body(): lax.all_gather(lined[1], 'gz', axis=3, tiled=True)  44.5 us
    all_gather x1, waiting for transfers between devices, body(): lax.all_gather(lined[2], 'gz', axis=3, tiled=True)  37.7 us
    reduce_scatter x1, waiting for transfers between devices, body(): lax.psum_scatter(jnp.dot(hidden, down_proj, preferred_element_type=jnp.fl...  37.5 us
    all_gather x1, waiting for transfers between devices, body(): lax.all_gather(normed, 'gz', axis=0, tiled=True)  33.1 us
  transfers between devices with their start and end apart: 12, of which 11 were waited for; matrix products, arithmetic and copies ran while one was open for 7% of the time, Pallas kernels for 0%

commit v1 on v0

--- a/solution.py
+++ b/solution.py
@@ -88,7 +88,9 @@
     normed = normalize(stream, gains[0])
     packed = jnp.dot(
         normed,
-        lax.all_gather(cross_qkv, "gx", axis=1, tiled=True),
+        jnp.concatenate(
+            lax.all_to_all(jnp.stack([cross_qkv] * lax.axis_size("gx")), "gx", 0, 0), axis=1
+        ),
         preferred_element_type=jnp.float32,
     ).astype(jnp.bfloat16)
     packed = packed.reshape(inlines, cross_dev, depth_dev, 3, head_count, HDIM)

time: 773 us -> 699 us (0.904)
  waiting for transfers between devices: 649 us -> 539 us
  starting transfers between devices: 23.1 us -> 55.1 us
    all_to_all x0 -> x1, waiting for transfers between devices: none -> 168 us  [body(): lax.all_to_all(jnp.stack([cross_qkv] * lax.axis_size('gx')), 'gx', 0, 0)]
    all_gather x1 -> x0, waiting for transfers between devices: 132 us -> none  [body(): lax.all_gather(cross_qkv, 'gx', axis=1, tiled=True)]
    all_gather x1, waiting for transfers between devices: 143 us -> 47.9 us  [body(): lax.all_gather(depth_qkv, 'gx', axis=1, tiled=True)]
    all_gather x1, waiting for transfers between devices: 49.5 us -> 0.02 us  [body(): lax.all_gather(cross_out, 'gx', axis=0, tiled=True)]
    all_to_all x0 -> x1, starting transfers between devices: none -> 19.5 us  [body(): lax.all_to_all(jnp.stack([cross_qkv] * lax.axis_size('gx')), 'gx', 0, 0)]
    unnamed x27 -> x26, local copies, waits for them, and re-layouts: 23.7 us -> 17.6 us
  transfers between devices with their start and end apart: 12 -> 12, of which waited for: 11 -> 10; matrix products, arithmetic and copies ran while one was open for 7% -> 8% of each run, Pallas kernels for 0% -> 0%
where the time goes in v1:
time: 699 us; the launch traced here: 698 us
  waiting for transfers between devices  539 us (77%)
  starting transfers between devices  55.1 us (8%)
  local copies, waits for them, and re-layouts  44.9 us (6%)
  matrix products  24.6 us (4%)
  between operations  15.2 us (2%)
  blocking collectives  13.4 us (2%)
    all_to_all x1, waiting for transfers between devices, body(): lax.all_to_all(jnp.stack([cross_qkv] * lax.axis_size('gx')), 'gx', 0, 0)  168 us
    all_gather x1, waiting for transfers between devices, body(): lax.all_gather(depth_out, 'gx', axis=0, tiled=True)  123 us
    all_gather x1, waiting for transfers between devices, body(): lax.all_gather(depth_qkv, 'gx', axis=1, tiled=True)  47.9 us
    all_gather x1, waiting for transfers between devices, body(): lax.all_gather(lined[1], 'gz', axis=3, tiled=True)  44.5 us
    all_gather x1, waiting for transfers between devices, body(): lax.all_gather(lined[2], 'gz', axis=3, tiled=True)  37.7 us
    reduce_scatter x1, waiting for transfers between devices, body(): lax.psum_scatter(jnp.dot(hidden, down_proj, preferred_element_type=jnp.fl...  37.5 us
    all_gather x1, waiting for transfers between devices, body(): lax.all_gather(normed, 'gz', axis=0, tiled=True)  33.1 us
    all_to_all x1, starting transfers between devices, body(): lax.all_to_all(jnp.stack([cross_qkv] * lax.axis_size('gx')), 'gx', 0, 0)  19.5 us
  transfers between devices with their start and end apart: 12, of which 10 were waited for; matrix products, arithmetic and copies ran while one was open for 8% of the time, Pallas kernels for 0%

profile of v1, /device:TPU:1, one launch (start us, length us, event | category | flops | bytes accessed | tf_op | source)
XLA Modules:
  0.0 697.8 jit_solution(6174178854687835219)
XLA Ops:
  7.2 3.0 stack.5
  10.2 19.5 %all-to-all-start = ((bf16[64,768,36]{1,2,0:T(8,128)(2,1)}), bf16[64,768,36]{1,2,0:T(8,128)(2,1)}, u32[]{:S(2)}, u32[]{:S(2)}) async-start(bf16[64,768,36]{1,2,0:T(8,128)(2,1)} %stack.5), calls=%async_computation | async-start | bytes 7864320 | tf_op jit(solution)/shard_map/all_to_all | solution.py:92
  29.8 0.7 all-gather.19.cloned.1.call-update
  30.5 0.7 all-gather.21.cloned.1.call-update
  31.3 0.8 fusion.39
  32.1 6.4 copy.79
  38.5 4.4 copy.80
  43.2 167.7 %all-to-all-done = bf16[64,768,36]{1,2,0:T(8,128)(2,1)} async-done(((bf16[64,768,36]{1,2,0:T(8,128)(2,1)}), bf16[64,768,36]{1,2,0:T(8,128)(2,1)}, u32[]{:S(2)}, u32[]{:S(2)}) %all-to-all-start) | async-done | bytes 3538976 | tf_op jit(solution)/shard_map/all_to_all | solution.py:92
  210.9 6.2 reshape.159
  217.1 3.3 convolution_convert_fusion.1
  220.4 1.0 reshape.160
  221.4 1.1 fusion.51
  222.5 0.3 copy.83
  222.8 0.9 reshape.188
  223.7 12.1 %all-to-all-start.2 = ((bf16[64,2,768]{2,1,0:T(2,128)(2,1)}), bf16[64,2,768]{2,1,0:T(2,128)(2,1)S(1)}, u32[]{:S(2)}, u32[]{:S(2)}) async-start(bf16[64,2,768]{2,1,0:T(2,128)(2,1)} %reshape.188), calls=%async_computation.2 | async-start | bytes 393216 | tf_op jit(solution)/shard_map/all_to_all | solution.py:103
  235.8 0.3 copy.81
  236.1 0.9 reshape.186
  237.0 15.4 %all-to-all-done.2 = bf16[64,2,768]{2,1,0:T(2,128)(2,1)S(1)} async-done(((bf16[64,2,768]{2,1,0:T(2,128)(2,1)}), bf16[64,2,768]{2,1,0:T(2,128)(2,1)S(1)}, u32[]{:S(2)}, u32[]{:S(2)}) %all-to-all-start.2) | async-done | bytes 196640 | tf_op jit(solution)/shard_map/all_to_all | solution.py:103
  252.4 7.9 %all-to-all-start.1 = ((bf16[64,2,768]{2,1,0:T(2,128)(2,1)}), bf16[64,2,768]{2,1,0:T(2,128)(2,1)S(1)}, u32[]{:S(2)}, u32[]{:S(2)}) async-start(bf16[64,2,768]{2,1,0:T(2,128)(2,1)} %reshape.186), calls=%async_computation.1 | async-start | bytes 393216 | tf_op jit(solution)/shard_map/all_to_all | solution.py:102
  260.4 0.3 copy.87
  260.7 0.9 reshape.184
  261.6 15.3 %all-to-all-done.1 = bf16[64,2,768]{2,1,0:T(2,128)(2,1)S(1)} async-done(((bf16[64,2,768]{2,1,0:T(2,128)(2,1)}), bf16[64,2,768]{2,1,0:T(2,128)(2,1)S(1)}, u32[]{:S(2)}, u32[]{:S(2)}) %all-to-all-start.1) | async-done | bytes 196640 | tf_op jit(solution)/shard_map/all_to_all | solution.py:102
  276.9 7.9 %all-to-all-start.3 = ((bf16[64,2,768]{2,1,0:T(2,128)(2,1)}), bf16[64,2,768]{2,1,0:T(2,128)(2,1)S(1)}, u32[]{:S(2)}, u32[]{:S(2)}) async-start(bf16[64,2,768]{2,1,0:T(2,128)(2,1)} %reshape.184), calls=%async_computation.3 | async-start | bytes 393216 | tf_op jit(solution)/shard_map/all_to_all | solution.py:104
  284.8 0.7 all-gather.23.cloned.1.call-update
  285.5 0.3 reshape.189
  285.9 0.3 reshape.187
  286.3 14.6 %all-to-all-done.3 = bf16[64,2,768]{2,1,0:T(2,128)(2,1)S(1)} async-done(((bf16[64,2,768]{2,1,0:T(2,128)(2,1)}), bf16[64,2,768]{2,1,0:T(2,128)(2,1)S(1)}, u32[]{:S(2)}, u32[]{:S(2)}) %all-to-all-start.3) | async-done | bytes 196640 | tf_op jit(solution)/shard_map/all_to_all | solution.py:104
  301.4 1.8 fusion.53
  303.2 1.7 fusion.27
  304.9 0.3 copy.91
  305.2 1.0 reshape.190
  306.2 7.5 %all-to-all-start.4 = ((bf16[64,2,768]{2,1,0:T(2,128)(2,1)}), bf16[64,2,768]{2,1,0:T(2,128)(2,1)S(1)}, u32[]{:S(2)}, u32[]{:S(2)}) async-start(bf16[64,2,768]{2,1,0:T(2,128)(2,1)} %reshape.190), calls=%async_computation.4 | async-start | bytes 393216 | tf_op jit(solution)/shard_map/all_to_all | solution.py:107
  313.8 2.3 reshape.174
  316.1 47.9 %all-gather.21.cloned.1.call-done = bf16[64,36,768]{2,1,0:T(8,128)(2,1)} async-done(((bf16[1,36,768]{2,1,0:T(8,128)(2,1)}), bf16[64,36,768]{2,1,0:T(8,128)(2,1)}) %all-gather.21.cloned.1.call-update) | async-done | bytes 3538960 | tf_op jit(solution)/shard_map/all_gather | solution.py:120
  364.0 6.2 reshape.176
  370.1 0.3 reshape.191
  370.7 0.3 reshape.165
  371.0 0.4 multiply_reduce_fusion.1
  371.5 0.7 copy-done.1
  372.2 3.3 convolution_convert_fusion
  375.5 1.0 reshape.166
  376.5 0.3 copy.106
  376.9 1.0 fusion.52
  377.9 0.5 all-gather.17.cloned.1.call-update
  378.5 122.9 %all-gather.23.cloned.1.call-done = bf16[64,12,768]{2,1,0:T(8,128)(2,1)} async-done(((bf16[1,12,768]{2,1,0:T(8,128)(2,1)}), bf16[64,12,768]{2,1,0:T(8,128)(2,1)}) %all-gather.23.cloned.1.call-update) | async-done | bytes 1179664 | tf_op jit(solution)/shard_map/all_gather | solution.py:134
  501.4 2.2 reshape.178
  503.6 44.5 %all-gather.15.cloned.1.call-done = bf16[1,4,4,12,64,64]{5,4,3,2,1,0:T(8,128)(2,1)} async-done(((bf16[1,4,4,12,8,64]{5,4,3,2,1,0:T(8,128)(2,1)}), bf16[1,4,4,12,64,64]{5,4,3,2,1,0:T(8,128)(2,1)}) %all-gather.15.cloned.1.call-update) | async-done | bytes 1572880 | tf_op jit(solution)/shard_map/all_gather | solution.py:126
  548.1 4.6 fusion.54
  552.7 37.7 %all-gather.17.cloned.1.call-done = bf16[1,4,4,12,64,64]{5,4,3,2,1,0:T(8,128)(2,1)} async-done(((bf16[1,4,4,12,8,64]{5,4,3,2,1,0:T(8,128)(2,1)}), bf16[1,4,4,12,64,64]{5,4,3,2,1,0:T(8,128)(2,1)}) %all-gather.17.cloned.1.call-update) | async-done | bytes 1572880 | tf_op jit(solution)/shard_map/all_gather | solution.py:127
  590.5 3.1 fusion.24
  593.7 0.3 reshape.167
  594.0 0.6 copy-done.2
  594.6 0.4 multiply_reduce_fusion
  595.0 0.8 multiply_convert_fusion
  595.9 33.1 %all-gather.13.cloned.1.call-done = bf16[1024,768]{1,0:T(8,128)(2,1)} async-done(((bf16[128,768]{1,0:T(8,128)(2,1)}), bf16[1024,768]{1,0:T(8,128)(2,1)}) %all-gather.13.cloned.1.call-update) | async-done | bytes 1572880 | tf_op jit(solution)/shard_map/all_gather | solution.py:140
  629.0 4.6 convolution_convert_fusion.2
  633.7 0.7 copy-done.6
  635.0 37.5 %reduce-scatter.2.cloned.1.call-done = bf16[128,768]{1,0:T(8,128)(2,1)} async-done(((bf16[1024,768]{1,0:T(8,128)(2,1)}), bf16[128,768]{1,0:T(8,128)(2,1)}) %reduce-scatter.2.cloned.1.call-update) | async-done | bytes 196624 | tf_op jit(solution)/shard_map/reduce_scatter | solution.py:145
  672.5 1.4 compare_select_fusion
  674.0 0.7 reduce_window_sum.11
  674.9 13.4 %all-gather.2 = f32[32,4,1]{1,2,0:T(1,128)S(1)} all-gather(f32[4,4,1]{1,2,0:T(1,128)S(1)} %copy.97), channel_id=4, replica_groups=mesh['gx'=64,'gz'=8] {'gz'}, dimensions={0}, use_global_device_ids=true | all-gather | bytes 576 | tf_op jit(solution)/shard_map/all_gather | solution.py:13
  688.3 0.3 while.14
  688.6 0.7 broadcast_add_fusion
  689.3 1.6 fusion.35
  (55 shorter events, 2.2 us)
Async XLA Ops:
  7.2 621.9 %copy-start = (bf16[384,768]{1,0:T(8,128)(2,1)S(1)}, bf16[384,768]{1,0:T(8,128)(2,1)}, u32[]{:S(2)}) copy-start(bf16[384,768]{1,0:T(8,128)(2,1)} %param.18) | copy-start | bytes 1769476
  10.2 200.7 %all-to-all-start = ((bf16[64,768,36]{1,2,0:T(8,128)(2,1)}), bf16[64,768,36]{1,2,0:T(8,128)(2,1)}, u32[]{:S(2)}, u32[]{:S(2)}) async-start(bf16[64,768,36]{1,2,0:T(8,128)(2,1)} %stack.5), calls=%async_computation | async-start | bytes 7864320 | tf_op jit(solution)/shard_map/all_to_all | solution.py:92
  29.7 284.1 %all-gather.19.cloned.1.call-start = ((), (), s32[]{:S(2)}) async-start(), calls=%async_computation.10 | async-start | bytes 1597440 | tf_op jit(solution)/shard_map/all_gather | solution.py:114
  30.4 333.5 %all-gather.21.cloned.1.call-start = ((), (), s32[]{:S(2)}) async-start(), calls=%async_computation.11 | async-start | bytes 3993600 | tf_op jit(solution)/shard_map/all_gather | solution.py:120
  38.5 4.4 copy-start.5
  38.5 4.4 copy-start.4
  222.5 13.3 %copy-start.3 = (bf16[1,4,8,12,4,64]{5,3,0,2,4,1:T(8,128)(2,1)S(1)}, bf16[1,4,8,12,4,64]{5,3,0,2,4,1:T(8,128)(2,1)}, u32[]{:S(2)}) copy-start(bf16[1,4,8,12,4,64]{5,3,0,2,4,1:T(8,128)(2,1)} %get-tuple-element.132) | copy-start | bytes 589828
  223.7 28.7 %all-to-all-start.2 = ((bf16[64,2,768]{2,1,0:T(2,128)(2,1)}), bf16[64,2,768]{2,1,0:T(2,128)(2,1)S(1)}, u32[]{:S(2)}, u32[]{:S(2)}) async-start(bf16[64,2,768]{2,1,0:T(2,128)(2,1)} %reshape.188), calls=%async_computation.2 | async-start | bytes 393216 | tf_op jit(solution)/shard_map/all_to_all | solution.py:103
  252.4 24.4 %all-to-all-start.1 = ((bf16[64,2,768]{2,1,0:T(2,128)(2,1)}), bf16[64,2,768]{2,1,0:T(2,128)(2,1)S(1)}, u32[]{:S(2)}, u32[]{:S(2)}) async-start(bf16[64,2,768]{2,1,0:T(2,128)(2,1)} %reshape.186), calls=%async_computation.1 | async-start | bytes 393216 | tf_op jit(solution)/shard_map/all_to_all | solution.py:102
  276.9 24.1 %all-to-all-start.3 = ((bf16[64,2,768]{2,1,0:T(2,128)(2,1)}), bf16[64,2,768]{2,1,0:T(2,128)(2,1)S(1)}, u32[]{:S(2)}, u32[]{:S(2)}) async-start(bf16[64,2,768]{2,1,0:T(2,128)(2,1)} %reshape.184), calls=%async_computation.3 | async-start | bytes 393216 | tf_op jit(solution)/shard_map/all_to_all | solution.py:104
  284.7 216.6 %all-gather.23.cloned.1.call-start = ((), (), s32[]{:S(2)}) async-start(), calls=%async_computation.12 | async-start | bytes 1597440 | tf_op jit(solution)/shard_map/all_gather | solution.py:134
  306.2 63.9 %all-to-all-start.4 = ((bf16[64,2,768]{2,1,0:T(2,128)(2,1)}), bf16[64,2,768]{2,1,0:T(2,128)(2,1)S(1)}, u32[]{:S(2)}, u32[]{:S(2)}) async-start(bf16[64,2,768]{2,1,0:T(2,128)(2,1)} %reshape.190), calls=%async_computation.4 | async-start | bytes 393216 | tf_op jit(solution)/shard_map/all_to_all | solution.py:107
  313.7 234.4 %all-gather.15.cloned.1.call-start = ((), (), s32[]{:S(2)}) async-start(), calls=%async_computation.8 | async-start | bytes 3538944 | tf_op jit(solution)/shard_map/all_gather | solution.py:126
  371.5 0.8 copy-start.1
  377.9 212.6 %all-gather.17.cloned.1.call-start = ((), (), s32[]{:S(2)}) async-start(), calls=%async_computation.9 | async-start | bytes 3538944 | tf_op jit(solution)/shard_map/all_gather | solution.py:127
  378.5 250.6 %all-gather.13.cloned.1.call-start = ((), (), s32[]{:S(2)}) async-start(), calls=%async_computation.6 | async-start | bytes 1769472 | tf_op jit(solution)/shard_map/all_gather | solution.py:140
  593.6 1.0 copy-start.2
  595.8 76.7 %reduce-scatter.2.cloned.1.call-start = ((), (), s32[]{:S(2)}) async-start(), calls=%async_computation.7 | async-start | bytes 1769472 | tf_op jit(solution)/shard_map/reduce_scatter | solution.py:145
  633.7 0.7 copy-start.6
Sparse Core Ops, SparseCore 0:
  33.5 180.3 all-gather.18
  216.9 147.0 all-gather.20
  366.9 134.3 all-gather.22
  503.3 44.7 all-gather.14
  550.1 40.3 all-gather.16
  596.0 33.0 all-gather.12
  633.8 38.6 reduce-scatter.1
